TPU v7x, 512 devices: a whole 4x8x8 slice. The times are simulated.
512 devices in a mesh: sims: 32 (over z_lo, y, core), sites: 16 (over x, z_hi).
Axes of the slice: x: 4, y: 8, z: 8 (z_hi: 4, z_lo: 2; z = z_hi * 2 + z_lo), core: 2. Of those that a mesh axis runs over, the one named last changes fastest.
Arguments:
- genotypes: int32 [32, 64, 8192], P('sims', None, 'sites'), may hold values from 0 to 1
- key_prior: bfloat16 [32, 2048], P('sims', 'sites'), may hold values from -300 to 300
- band_reach: int32 [32], P('sims'), may hold values from 128 to 512, as said below
- cotangent: bfloat16 [32, 2048, 512], P('sims', 'sites'), may hold values from -0.09375 to 0.09375
- conv_weight: float32 [4, 64], replicated, may hold values from -3 to 3
- conv_bias: float32 [64], replicated, may hold values from -3 to 3
- mix_weight: float32 [3, 64, 64], replicated, may hold values from -0.4375 to 0.4375
- embed_weight: float32 [64, 512], replicated, may hold values from -0.75 to 0.75
- norm_gain: float32 [512], replicated, may hold values from 0.5 to 1.5
- attn_weight: bfloat16 [4, 512, 512], replicated, may hold values from -0.25 to 0.25
Outputs:
- grad_attention: float32 [1048576], P(('sims', 'sites'))
- grad_conv: float32 [4, 64], replicated
- grad_bias: float32 [64], replicated
- grad_mix: float32 [3, 64, 64], replicated
- grad_embed: float32 [64, 512], replicated
- grad_gain: float32 [512], replicated
Inputs may be any that keep to these rules, and one draw needn't show every extreme that they name: `band_reach`: some evolution has reach exactly 512 in every draw.
All inputs are finite; a program needn't handle non-finite values.
Results may differ from a plain program's by a relative error of at most 0.017.
Values may be sent and summed in bfloat16 or wider, within the bound.
A program may use at most 64 MiB of HBM per device.

v0:
```python
import jax
import jax.numpy as jnp
from jax import lax
from jax.sharding import PartitionSpec as P

HEADS = 8
HEAD_DIM = 64
BAND = 512
HIGH = lax.Precision.HIGHEST
EPS = 1e-06


def extended(cells, sides, width):
    for axis, dim in sides:
        count = lax.axis_size(axis)
        head = lax.slice_in_dim(cells, 0, width, axis=dim)
        tail = lax.slice_in_dim(cells, cells.shape[dim] - width, cells.shape[dim], axis=dim)
        cells = jnp.concatenate(
            [
                lax.ppermute(tail, axis, [(i, (i + 1) % count) for i in range(count)]),
                cells,
                lax.ppermute(head, axis, [((i + 1) % count, i) for i in range(count)]),
            ],
            axis=dim,
        )
    return cells


def from_behind(value, axis, steps):
    count = lax.axis_size(axis)
    pairs = [(source, (source + steps) % count) for source in range(count)]
    return lax.ppermute(value, axis, pairs)


def silu_slope(value):
    sigma = jax.nn.sigmoid(value)
    return sigma * (1.0 + value * (1.0 - sigma))


def block_offsets(count, reach_blocks):
    chosen = []
    taken = []
    for distance in range(reach_blocks + 1):
        for offset in (distance, -distance):
            if offset % count not in taken:
                taken.append(offset % count)
                chosen.append(offset)
    return chosen


def split_heads(array, heads):
    return array.reshape(array.shape[0], array.shape[1], heads, array.shape[2] // heads)


def band_scores(query, keys, prior, query_places, key_places, limit, cycle_tokens, factor):
    scores = jnp.einsum("sqhe,skhe->shqk", query, keys, preferred_element_type=jnp.float32) * factor
    scores = scores + prior.astype(jnp.float32)[:, None, None, :]
    apart = (key_places[None, :] - query_places[:, None]) % cycle_tokens
    apart = jnp.minimum(apart, cycle_tokens - apart)
    inside = apart[None, None] <= limit[:, None, None, None]
    return (scores, inside)


def per_device(
    genotypes,
    key_prior,
    band_reach,
    cotangent,
    conv_weight,
    conv_bias,
    mix_weight,
    embed_weight,
    norm_gain,
    attn_weight,
):
    sims, haps, sites = genotypes.shape
    patch = conv_weight.shape[0]
    local = sites // patch
    width = attn_weight.shape[1]
    heads = HEADS
    factor = HEAD_DIM ** (-0.5)
    count = lax.axis_size("sites")
    cycle_tokens = local * count
    place = lax.axis_index("sites")
    ordinal = jnp.arange(local, dtype=jnp.int32)
    patches = genotypes.astype(jnp.float32).reshape(sims, haps, local, patch)
    pre = (
        jnp.einsum("shtk,kc->shct", patches, conv_weight, precision=HIGH)
        + conv_bias[None, None, :, None]
    )
    pooled = jnp.mean(jax.nn.silu(pre), axis=1)
    pooled_wide = extended(pooled, (("sites", 2),), 1)
    mixed = jnp.zeros((sims, mix_weight.shape[2], local), jnp.float32)
    for shift_by in (-1, 0, 1):
        mixed = mixed + jnp.einsum(
            "co,sct->sot",
            mix_weight[shift_by + 1],
            pooled_wide[:, :, 1 + shift_by : 1 + shift_by + local],
            precision=HIGH,
        )
    activated = jax.nn.silu(mixed)
    embedded = jnp.einsum("sct,cd->std", activated, embed_weight, precision=HIGH).astype(
        jnp.bfloat16
    )
    wide = embedded.astype(jnp.float32)
    inverse = lax.rsqrt(jnp.mean(wide * wide, axis=2, keepdims=True) + EPS)
    normed = (wide * inverse * norm_gain).astype(jnp.bfloat16)
    query = jnp.einsum(
        "std,de->ste", normed, attn_weight[0], preferred_element_type=jnp.float32
    ).astype(jnp.bfloat16)
    keys = jnp.einsum(
        "std,de->ste", normed, attn_weight[1], preferred_element_type=jnp.float32
    ).astype(jnp.bfloat16)
    values = jnp.einsum(
        "std,de->ste", normed, attn_weight[2], preferred_element_type=jnp.float32
    ).astype(jnp.bfloat16)
    query_heads = split_heads(query, heads)
    key_heads = split_heads(keys, heads)
    value_heads = split_heads(values, heads)
    reach_blocks = -(-BAND // local)
    offsets = block_offsets(count, reach_blocks)
    packed = jnp.concatenate([keys, values, key_prior[:, :, None]], axis=2)
    gathered = {0: packed}
    for offset in offsets[1:]:
        gathered[offset] = from_behind(packed, "sites", -offset)
    packed_cat = jnp.concatenate([gathered[offset] for offset in offsets], axis=1)
    key_cat = split_heads(packed_cat[:, :, :width], heads)
    value_cat = split_heads(packed_cat[:, :, width : 2 * width], heads)
    prior_cat = packed_cat[:, :, 2 * width]
    key_places = jnp.concatenate([(place + offset) % count * local + ordinal for offset in offsets])
    query_places = place * local + ordinal
    scores, inside = band_scores(
        query_heads, key_cat, prior_cat, query_places, key_places, band_reach, cycle_tokens, factor
    )
    row_top = jnp.max(jnp.where(inside, scores, -jnp.inf), axis=-1, keepdims=True)
    lifted = jnp.where(inside, jnp.exp(scores - row_top), 0.0)
    row_total = jnp.sum(lifted, axis=-1, keepdims=True)
    prob = lifted / row_total
    prob_half = prob.astype(jnp.bfloat16)
    attended_full = jnp.einsum(
        "shqk,skhe->sqhe", prob_half, value_cat, preferred_element_type=jnp.float32
    )
    attended = attended_full.astype(jnp.bfloat16).reshape(sims, local, width)
    grad_attended = jnp.einsum(
        "std,ed->ste", cotangent, attn_weight[3], preferred_element_type=jnp.float32
    ).astype(jnp.bfloat16)
    grad_heads = split_heads(grad_attended, heads)
    delta = jnp.einsum("sqhe,sqhe->shq", grad_heads.astype(jnp.float32), attended_full)
    grad_prob = jnp.einsum(
        "sqhe,skhe->shqk", grad_heads, value_cat, preferred_element_type=jnp.float32
    )
    grad_scores = (prob * (grad_prob - delta[..., None]) * factor).astype(jnp.bfloat16)
    grad_query = jnp.einsum(
        "shqk,skhe->sqhe", grad_scores, key_cat, preferred_element_type=jnp.float32
    ).astype(jnp.bfloat16)
    grad_query = grad_query.reshape(sims, local, width)
    key_part = jnp.einsum(
        "shqk,sqhe->skhe", grad_scores, query_heads, preferred_element_type=jnp.float32
    )
    value_part = jnp.einsum(
        "shqk,sqhe->skhe", prob_half, grad_heads, preferred_element_type=jnp.float32
    )
    key_sum = key_part[:, 0:local]
    value_sum = value_part[:, 0:local]
    for position, offset in enumerate(offsets[1:], start=1):
        lower = position * local
        both = jnp.concatenate(
            [key_part[:, lower : lower + local], value_part[:, lower : lower + local]], axis=2
        ).astype(jnp.bfloat16)
        back = from_behind(both, "sites", offset).astype(jnp.float32)
        key_sum = key_sum + back[:, :, :heads]
        value_sum = value_sum + back[:, :, heads:]
    grad_keys = key_sum.astype(jnp.bfloat16).reshape(sims, local, width)
    grad_values = value_sum.astype(jnp.bfloat16).reshape(sims, local, width)
    term_query = jnp.einsum("std,ste->de", normed, grad_query, preferred_element_type=jnp.float32)
    term_keys = jnp.einsum("std,ste->de", normed, grad_keys, preferred_element_type=jnp.float32)
    term_values = jnp.einsum("std,ste->de", normed, grad_values, preferred_element_type=jnp.float32)
    term_output = jnp.einsum("std,ste->de", attended, cotangent, preferred_element_type=jnp.float32)
    flat_terms = jnp.stack([term_query, term_keys, term_values, term_output]).reshape(-1)
    grad_attention = lax.psum_scatter(
        lax.psum_scatter(flat_terms, "sims", scatter_dimension=0, tiled=True),
        "sites",
        scatter_dimension=0,
        tiled=True,
    )
    grad_normed = jnp.einsum(
        "ste,de->std", grad_query, attn_weight[0], preferred_element_type=jnp.float32
    )
    grad_normed = grad_normed + jnp.einsum(
        "ste,de->std", grad_keys, attn_weight[1], preferred_element_type=jnp.float32
    )
    grad_normed = grad_normed + jnp.einsum(
        "ste,de->std", grad_values, attn_weight[2], preferred_element_type=jnp.float32
    )
    term_gain = jnp.sum(grad_normed * wide * inverse, axis=(0, 1))
    scaled = grad_normed * norm_gain
    grad_embedded = (
        inverse * scaled - wide * inverse**3 * jnp.sum(scaled * wide, axis=2, keepdims=True) / width
    )
    grad_embedded = grad_embedded + cotangent.astype(jnp.float32)
    term_embed = jnp.einsum("sct,std->cd", activated, grad_embedded, precision=HIGH)
    grad_mixed = jnp.einsum(
        "std,od->sot", grad_embedded, embed_weight, precision=HIGH
    ) * silu_slope(mixed)
    mixed_wide = extended(grad_mixed.astype(jnp.bfloat16), (("sites", 2),), 1).astype(
        grad_mixed.dtype
    )
    mix_terms = []
    grad_pooled = jnp.zeros(pooled.shape, jnp.float32)
    for shift_by in (-1, 0, 1):
        mix_terms.append(
            jnp.einsum(
                "sct,sot->co",
                pooled_wide[:, :, 1 + shift_by : 1 + shift_by + local],
                grad_mixed,
                precision=HIGH,
            )
        )
        grad_pooled = grad_pooled + jnp.einsum(
            "co,sot->sct",
            mix_weight[shift_by + 1],
            mixed_wide[:, :, 1 - shift_by : 1 - shift_by + local],
            precision=HIGH,
        )
    grad_pre = (grad_pooled / haps)[:, None] * silu_slope(pre)
    term_conv = jnp.einsum("shtk,shct->kc", patches, grad_pre, precision=HIGH)
    term_bias = jnp.sum(grad_pre, axis=(0, 1, 3))
    small = (term_conv, term_bias, jnp.stack(mix_terms), term_embed, term_gain)
    flat_small = lax.psum(jnp.concatenate([t.reshape(-1) for t in small]), ("sims", "sites"))
    pieces = []
    lower = 0
    for t in small:
        pieces.append(flat_small[lower : lower + t.size].reshape(t.shape))
        lower += t.size
    grad_conv, grad_bias, grad_mix, grad_embed, grad_gain = pieces
    return (grad_attention, grad_conv, grad_bias, grad_mix, grad_embed, grad_gain)


def solution(mesh):
    placed = (
        P("sims", None, "sites"),
        P("sims", "sites"),
        P("sims"),
        P("sims", "sites", None),
        P(),
        P(),
        P(),
        P(),
        P(),
        P(),
    )
    return jax.shard_map(
        per_device,
        mesh=mesh,
        in_specs=placed,
        out_specs=(P(("sims", "sites")), P(), P(), P(), P(), P()),
        check_vma=False,
    )
```

profile of v0, /device:TPU:8, one launch (start us, length us, event | category | flops | bytes accessed | tf_op | source)
XLA Modules:
  0.0 869.0 jit_solution(17943417780981665908)
XLA Ops:
  8.5 4.5 fusion.16
  13.1 13.1 %collective-permute-start.1 = (f32[1,64,1]{2,1,0:T(8,128)S(1)}, f32[1,64,1]{2,1,0:T(8,128)S(1)}, u32[]{:S(2)}, u32[]{:S(2)}) collective-permute-start(f32[1,64,1]{2,1,0:T(8,128)S(1)} %get-tuple-element.31), channel_id=1, source_target_pairs={{1,0},{2,1},{3,2},{4,3},{5,4},{6,5},{7,6},{8,7},{9,8},{10,9},{11,1... | collective-permute-start | bytes 776 | tf_op jit(solution)/shard_map/ppermute | solution.py:22
  26.3 1.9 collective-permute-start
  30.2 6.0 collective-permute-done
  39.5 2.1 collective-permute-start.2
  42.0 4.6 collective-permute-start.3
  46.7 1.9 collective-permute-start.4
  48.6 7.8 collective-permute-start.5
  56.4 1.9 collective-permute-start.6
  58.7 9.6 %collective-permute-done.2 = bf16[1,128,1025]{2,1,0:T(8,128)(2,1)} collective-permute-done((bf16[1,128,1025]{2,1,0:T(8,128)(2,1)}, bf16[1,128,1025]{2,1,0:T(8,128)(2,1)}, u32[]{:S(2)}, u32[]{:S(2)}) %collective-permute-start.2) | collective-permute-done | bytes 262432 | tf_op jit(solution)/shard_map/ppermute | solution.py:32
  71.9 2.8 collective-permute-start.8
  76.4 3.8 collective-permute-done.4
  80.3 15.8 %collective-permute-start.9 = (bf16[1,128,1025]{2,1,0:T(8,128)(2,1)}, bf16[1,128,1025]{2,1,0:T(8,128)(2,1)S(1)}, u32[]{:S(2)}, u32[]{:S(2)}) collective-permute-start(bf16[1,128,1025]{2,1,0:T(8,128)(2,1)} %get-tuple-element.28), channel_id=1, source_target_pairs={{0,4},{1,5},{2,6},{3,7},{4,8},{5,9},{6,10},{7,11},{8,12},{9,13},{1... | collective-permute-start | bytes 787208 | tf_op jit(solution)/shard_map/ppermute | solution.py:32
  103.6 2.8 fusion.114
  118.3 6.1 collective-permute-start.10
  124.4 4.0 collective-permute-start.11
  128.5 4.2 collective-permute-start.12
  132.7 7.7 collective-permute-start.13
  140.4 1.9 collective-permute-start.14
  142.5 6.9 collective-permute-start.15
  149.4 2.3 collective-permute-start.16
  151.7 4.8 collective-permute-start.17
  158.2 2.1 collective-permute-done.13
  160.4 4.4 collective-permute-done.14
  166.6 3.1 copy.52
  174.2 9.6 %collective-permute-start.19 = (bf16[1,64,1]{2,1,0:T(8,128)(2,1)S(1)}, bf16[1,64,1]{2,1,0:T(8,128)(2,1)S(1)}, u32[]{:S(2)}, u32[]{:S(2)}) collective-permute-start(bf16[1,64,1]{2,1,0:T(8,128)(2,1)S(1)} %get-tuple-element.33), channel_id=1, source_target_pairs={{0,1},{1,2},{2,3},{3,4},{4,5},{5,6},{6,7},{7,8},{8,9},{9,10},{10,1... | collective-permute-start | bytes 392 | tf_op jit(solution)/shard_map/ppermute | solution.py:20
  184.0 1.9 collective-permute-start.18
  186.1 4.4 collective-permute-done.18
  190.8 2.4 fusion.30
  197.0 225.5 %all-reduce.8.cloned.1.call-done = f32[1048576]{0:T(1024)} async-done(((f32[1048576]{0:T(1024)}), f32[1048576]{0:T(1024)}) %all-reduce.8.cloned.1.call-update) | async-done | bytes 4194320
  426.0 267.0 %all-reduce.6.cloned.1.call-done = f32[45888]{0:T(1024)} async-done(((f32[45888]{0:T(1024)}), f32[45888]{0:T(1024)}) %all-reduce.6.cloned.1.call-update) | async-done | bytes 183568 | tf_op jit(solution)/shard_map/psum | solution.py:229
  700.2 161.0 %all-reduce.10.cloned.1.call-done = f32[32768]{0:T(1024)} async-done(((f32[32768]{0:T(1024)}), f32[32768]{0:T(1024)}) %all-reduce.10.cloned.1.call-update) | async-done | bytes 131088
  (162 shorter events, 54.2 us)
Async XLA Ops:
  7.2 29.4 %copy-start = (f32[64,512]{1,0:T(8,128)S(1)}, f32[64,512]{1,0:T(8,128)}, u32[]{:S(2)}) copy-start(f32[64,512]{1,0:T(8,128)} %param.17) | copy-start | bytes 393220
  7.2 415.3 %all-reduce.8.cloned.1.call-start = ((), (), s32[]{:S(2)}) async-start(), calls=%async_computation.1 | async-start | bytes 8388608
  8.5 21.1 %copy-start.5 = (f32[3,64,64]{2,1,0:T(8,128)S(1)}, f32[3,64,64]{2,1,0:T(8,128)}, u32[]{:S(2)}) copy-start(f32[3,64,64]{2,1,0:T(8,128)} %param.16) | copy-start | bytes 147460
  8.5 21.4 %copy-start.15 = (bf16[1,128]{1,0:T(2,128)(2,1)S(1)}, bf16[1,128]{1,0:T(2,128)(2,1)}, u32[]{:S(2)}) copy-start(bf16[1,128]{1,0:T(2,128)(2,1)} %param.11) | copy-start | bytes 772
  8.5 29.1 %copy-start.11 = (f32[512]{0:T(512)S(1)}, f32[512]{0:T(512)}, u32[]{:S(2)}) copy-start(f32[512]{0:T(512)} %param.18) | copy-start | bytes 6148
  8.5 29.6 %copy-start.1 = (bf16[4,512,512]{2,1,0:T(8,128)(2,1)S(1)}, bf16[4,512,512]{2,1,0:T(8,128)(2,1)}, u32[]{:S(2)}) copy-start(bf16[4,512,512]{2,1,0:T(8,128)(2,1)} %param.19) | copy-start | bytes 6291460
  13.1 28.5 %copy-start.4 = (bf16[1,128,512]{2,1,0:T(8,128)(2,1)S(1)}, bf16[1,128,512]{2,1,0:T(8,128)(2,1)}, u32[]{:S(2)}) copy-start(bf16[1,128,512]{2,1,0:T(8,128)(2,1)} %param.13) | copy-start | bytes 393220
  13.1 16.8 %collective-permute-start.1 = (f32[1,64,1]{2,1,0:T(8,128)S(1)}, f32[1,64,1]{2,1,0:T(8,128)S(1)}, u32[]{:S(2)}, u32[]{:S(2)}) collective-permute-start(f32[1,64,1]{2,1,0:T(8,128)S(1)} %get-tuple-element.31), channel_id=1, source_target_pairs={{1,0},{2,1},{3,2},{4,3},{5,4},{6,5},{7,6},{8,7},{9,8},{10,9},{11,1... | collective-permute-start | bytes 776 | tf_op jit(solution)/shard_map/ppermute | solution.py:22
  26.3 10.0 %collective-permute-start = (f32[1,64,1]{2,1,0:T(8,128)S(1)}, f32[1,64,1]{2,1,0:T(8,128)S(1)}, u32[]{:S(2)}, u32[]{:S(2)}) collective-permute-start(f32[1,64,1]{2,1,0:T(8,128)S(1)} %get-tuple-element.30), channel_id=1, source_target_pairs={{0,1},{1,2},{2,3},{3,4},{4,5},{5,6},{6,7},{7,8},{8,9},{9,10},{10,1... | collective-permute-start | bytes 776 | tf_op jit(solution)/shard_map/ppermute | solution.py:20
  39.5 28.8 %collective-permute-start.2 = (bf16[1,128,1025]{2,1,0:T(8,128)(2,1)}, bf16[1,128,1025]{2,1,0:T(8,128)(2,1)}, u32[]{:S(2)}, u32[]{:S(2)}) collective-permute-start(bf16[1,128,1025]{2,1,0:T(8,128)(2,1)} %get-tuple-element.28), channel_id=1, source_target_pairs={{0,15},{1,0},{2,1},{3,2},{4,3},{5,4},{6,5},{7,6},{8,7},{9,8},{10,9... | collective-permute-start | bytes 787208 | tf_op jit(solution)/shard_map/ppermute | solution.py:32
  42.0 29.9 %collective-permute-start.3 = (bf16[1,128,1025]{2,1,0:T(8,128)(2,1)}, bf16[1,128,1025]{2,1,0:T(8,128)(2,1)}, u32[]{:S(2)}, u32[]{:S(2)}) collective-permute-start(bf16[1,128,1025]{2,1,0:T(8,128)(2,1)} %get-tuple-element.28), channel_id=1, source_target_pairs={{0,1},{1,2},{2,3},{3,4},{4,5},{5,6},{6,7},{7,8},{8,9},{9,10},{10,1... | collective-permute-start | bytes 787208 | tf_op jit(solution)/shard_map/ppermute | solution.py:32
  46.7 33.6 %collective-permute-start.4 = (bf16[1,128,1025]{2,1,0:T(8,128)(2,1)}, bf16[1,128,1025]{2,1,0:T(8,128)(2,1)}, u32[]{:S(2)}, u32[]{:S(2)}) collective-permute-start(bf16[1,128,1025]{2,1,0:T(8,128)(2,1)} %get-tuple-element.28), channel_id=1, source_target_pairs={{0,14},{1,15},{2,0},{3,1},{4,2},{5,3},{6,4},{7,5},{8,6},{9,7},{10,... | collective-permute-start | bytes 787208 | tf_op jit(solution)/shard_map/ppermute | solution.py:32
  48.6 49.2 %collective-permute-start.5 = (bf16[1,128,1025]{2,1,0:T(8,128)(2,1)}, bf16[1,128,1025]{2,1,0:T(8,128)(2,1)}, u32[]{:S(2)}, u32[]{:S(2)}) collective-permute-start(bf16[1,128,1025]{2,1,0:T(8,128)(2,1)} %get-tuple-element.28), channel_id=1, source_target_pairs={{0,2},{1,3},{2,4},{3,5},{4,6},{5,7},{6,8},{7,9},{8,10},{9,11},{10,... | collective-permute-start | bytes 787208 | tf_op jit(solution)/shard_map/ppermute | solution.py:32
  56.4 43.0 %collective-permute-start.6 = (bf16[1,128,1025]{2,1,0:T(8,128)(2,1)}, bf16[1,128,1025]{2,1,0:T(8,128)(2,1)}, u32[]{:S(2)}, u32[]{:S(2)}) collective-permute-start(bf16[1,128,1025]{2,1,0:T(8,128)(2,1)} %get-tuple-element.28), channel_id=1, source_target_pairs={{0,13},{1,14},{2,15},{3,0},{4,1},{5,2},{6,3},{7,4},{8,5},{9,6},{10... | collective-permute-start | bytes 787208 | tf_op jit(solution)/shard_map/ppermute | solution.py:32
  68.3 32.9 %collective-permute-start.7 = (bf16[1,128,1025]{2,1,0:T(8,128)(2,1)}, bf16[1,128,1025]{2,1,0:T(8,128)(2,1)S(1)}, u32[]{:S(2)}, u32[]{:S(2)}) collective-permute-start(bf16[1,128,1025]{2,1,0:T(8,128)(2,1)} %get-tuple-element.28), channel_id=1, source_target_pairs={{0,3},{1,4},{2,5},{3,6},{4,7},{5,8},{6,9},{7,10},{8,11},{9,12},{10... | collective-permute-start | bytes 787208 | tf_op jit(solution)/shard_map/ppermute | solution.py:32
  71.9 30.0 %collective-permute-start.8 = (bf16[1,128,1025]{2,1,0:T(8,128)(2,1)}, bf16[1,128,1025]{2,1,0:T(8,128)(2,1)S(1)}, u32[]{:S(2)}, u32[]{:S(2)}) collective-permute-start(bf16[1,128,1025]{2,1,0:T(8,128)(2,1)} %get-tuple-element.28), channel_id=1, source_target_pairs={{0,12},{1,13},{2,14},{3,15},{4,0},{5,1},{6,2},{7,3},{8,4},{9,5},{1... | collective-permute-start | bytes 787208 | tf_op jit(solution)/shard_map/ppermute | solution.py:32
  80.3 22.6 %collective-permute-start.9 = (bf16[1,128,1025]{2,1,0:T(8,128)(2,1)}, bf16[1,128,1025]{2,1,0:T(8,128)(2,1)S(1)}, u32[]{:S(2)}, u32[]{:S(2)}) collective-permute-start(bf16[1,128,1025]{2,1,0:T(8,128)(2,1)} %get-tuple-element.28), channel_id=1, source_target_pairs={{0,4},{1,5},{2,6},{3,7},{4,8},{5,9},{6,10},{7,11},{8,12},{9,13},{1... | collective-permute-start | bytes 787208 | tf_op jit(solution)/shard_map/ppermute | solution.py:32
  118.3 24.1 %collective-permute-start.10 = (bf16[1,128,16,64]{1,3,2,0:T(8,128)(2,1)S(1)}, bf16[1,128,16,64]{1,3,2,0:T(8,128)(2,1)S(1)}, u32[]{:S(2)}, u32[]{:S(2)}) collective-permute-start(bf16[1,128,16,64]{1,3,2,0:T(8,128)(2,1)S(1)} %pad_maximum_fusion.2), channel_id=1, source_target_pairs={{0,1},{1,2},{2,3},{3,4},{4,5},{5,6},{6,7},{7,8},{8,9},{9,10},{10,1... | collective-permute-start | bytes 786440 | tf_op jit(solution)/shard_map/ppermute | solution.py:32
  124.4 25.0 %collective-permute-start.11 = (bf16[1,128,16,64]{1,3,2,0:T(8,128)(2,1)S(1)}, bf16[1,128,16,64]{1,3,2,0:T(8,128)(2,1)S(1)}, u32[]{:S(2)}, u32[]{:S(2)}) collective-permute-start(bf16[1,128,16,64]{1,3,2,0:T(8,128)(2,1)S(1)} %pad_maximum_fusion.3), channel_id=1, source_target_pairs={{0,15},{1,0},{2,1},{3,2},{4,3},{5,4},{6,5},{7,6},{8,7},{9,8},{10,9... | collective-permute-start | bytes 786440 | tf_op jit(solution)/shard_map/ppermute | solution.py:32
  128.5 23.2 %collective-permute-start.12 = (bf16[1,128,16,64]{1,3,2,0:T(8,128)(2,1)S(1)}, bf16[1,128,16,64]{1,3,2,0:T(8,128)(2,1)S(1)}, u32[]{:S(2)}, u32[]{:S(2)}) collective-permute-start(bf16[1,128,16,64]{1,3,2,0:T(8,128)(2,1)S(1)} %pad_maximum_fusion.4), channel_id=1, source_target_pairs={{0,2},{1,3},{2,4},{3,5},{4,6},{5,7},{6,8},{7,9},{8,10},{9,11},{10,... | collective-permute-start | bytes 786440 | tf_op jit(solution)/shard_map/ppermute | solution.py:32
  132.7 27.7 %collective-permute-start.13 = (bf16[1,128,16,64]{1,3,2,0:T(8,128)(2,1)S(1)}, bf16[1,128,16,64]{1,3,2,0:T(8,128)(2,1)S(1)}, u32[]{:S(2)}, u32[]{:S(2)}) collective-permute-start(bf16[1,128,16,64]{1,3,2,0:T(8,128)(2,1)S(1)} %pad_maximum_fusion.5), channel_id=1, source_target_pairs={{0,14},{1,15},{2,0},{3,1},{4,2},{5,3},{6,4},{7,5},{8,6},{9,7},{10,... | collective-permute-start | bytes 786440 | tf_op jit(solution)/shard_map/ppermute | solution.py:32
  140.4 24.4 %collective-permute-start.14 = (bf16[1,128,16,64]{1,3,2,0:T(8,128)(2,1)S(1)}, bf16[1,128,16,64]{1,3,2,0:T(8,128)(2,1)S(1)}, u32[]{:S(2)}, u32[]{:S(2)}) collective-permute-start(bf16[1,128,16,64]{1,3,2,0:T(8,128)(2,1)S(1)} %pad_maximum_fusion.6), channel_id=1, source_target_pairs={{0,3},{1,4},{2,5},{3,6},{4,7},{5,8},{6,9},{7,10},{8,11},{9,12},{10... | collective-permute-start | bytes 786440 | tf_op jit(solution)/shard_map/ppermute | solution.py:32
  142.5 22.4 %collective-permute-start.15 = (bf16[1,128,16,64]{1,3,2,0:T(8,128)(2,1)S(1)}, bf16[1,128,16,64]{1,3,2,0:T(8,128)(2,1)S(1)}, u32[]{:S(2)}, u32[]{:S(2)}) collective-permute-start(bf16[1,128,16,64]{1,3,2,0:T(8,128)(2,1)S(1)} %pad_maximum_fusion.7), channel_id=1, source_target_pairs={{0,13},{1,14},{2,15},{3,0},{4,1},{5,2},{6,3},{7,4},{8,5},{9,6},{10... | collective-permute-start | bytes 786440 | tf_op jit(solution)/shard_map/ppermute | solution.py:32
  149.4 15.5 %collective-permute-start.16 = (bf16[1,128,16,64]{1,3,2,0:T(8,128)(2,1)S(1)}, bf16[1,128,16,64]{1,3,2,0:T(8,128)(2,1)S(1)}, u32[]{:S(2)}, u32[]{:S(2)}) collective-permute-start(bf16[1,128,16,64]{1,3,2,0:T(8,128)(2,1)S(1)} %pad_maximum_fusion.8), channel_id=1, source_target_pairs={{0,4},{1,5},{2,6},{3,7},{4,8},{5,9},{6,10},{7,11},{8,12},{9,13},{1... | collective-permute-start | bytes 786440 | tf_op jit(solution)/shard_map/ppermute | solution.py:32
  151.7 13.2 %collective-permute-start.17 = (bf16[1,128,16,64]{1,3,2,0:T(8,128)(2,1)S(1)}, bf16[1,128,16,64]{1,3,2,0:T(8,128)(2,1)S(1)}, u32[]{:S(2)}, u32[]{:S(2)}) collective-permute-start(bf16[1,128,16,64]{1,3,2,0:T(8,128)(2,1)S(1)} %pad_maximum_fusion.9), channel_id=1, source_target_pairs={{0,12},{1,13},{2,14},{3,15},{4,0},{5,1},{6,2},{7,3},{8,4},{9,5},{1... | collective-permute-start | bytes 786440 | tf_op jit(solution)/shard_map/ppermute | solution.py:32
  169.8 523.3 %all-reduce.6.cloned.1.call-start = ((), (), s32[]{:S(2)}) async-start(), calls=%async_computation | async-start | bytes 368640 | tf_op jit(solution)/shard_map/psum | solution.py:229
  172.0 18.8 %copy-start.8 = (f32[64,128,4]{1,2,0:T(4,128)S(1)}, f32[64,128,4]{1,2,0:T(4,128)}, u32[]{:S(2)}) copy-start(f32[64,128,4]{1,2,0:T(4,128)} %copy-done.7) | copy-start | bytes 393220
  172.0 18.8 %copy-start.17 = (f32[64]{0:T(128)S(1)}, f32[64]{0:T(128)}, u32[]{:S(2)}) copy-start(f32[64]{0:T(128)} %param.15) | copy-start | bytes 772
  172.4 18.3 %copy-start.3 = (f32[64,64,128]{2,0,1:T(8,128)S(1)}, f32[64,64,128]{2,0,1:T(8,128)}, u32[]{:S(2)}) copy-start(f32[64,64,128]{2,0,1:T(8,128)} %get-tuple-element.37) | copy-start | bytes 6291460
  174.2 11.7 %collective-permute-start.19 = (bf16[1,64,1]{2,1,0:T(8,128)(2,1)S(1)}, bf16[1,64,1]{2,1,0:T(8,128)(2,1)S(1)}, u32[]{:S(2)}, u32[]{:S(2)}) collective-permute-start(bf16[1,64,1]{2,1,0:T(8,128)(2,1)S(1)} %get-tuple-element.33), channel_id=1, source_target_pairs={{0,1},{1,2},{2,3},{3,4},{4,5},{5,6},{6,7},{7,8},{8,9},{9,10},{10,1... | collective-permute-start | bytes 392 | tf_op jit(solution)/shard_map/ppermute | solution.py:20
  184.0 6.5 collective-permute-start.18
  195.1 666.1 %all-reduce.10.cloned.1.call-start = ((), (), s32[]{:S(2)}) async-start(), calls=%async_computation.2 | async-start | bytes 262144
  (9 other events, 28.9 us)
Sparse Core Ops, SparseCore 0:
  169.9 252.5 all-reduce.7
  427.5 265.5 all-reduce.5
  696.2 164.9 all-reduce.9
where the time goes:
time: 870 us; the launch traced here: 869 us
  waiting for transfers between devices  684 us (79%)
  starting transfers between devices  104 us (12%)
  local copies, waits for them, and re-layouts  35.6 us (4%)
  matrix products  19.2 us (2%)
  between operations  16.8 us (2%)
  other arithmetic  9.7 us (1%)
    unnamed x5, waiting for transfers between devices  386 us
    psum x1, waiting for transfers between devices, per_device(): lax.psum(jnp.concatenate([t.reshape(-1) for t in small]), ('sims', 'sites'))  267 us
    ppermute x16, starting transfers between devices, from_behind(): return lax.ppermute(value, axis, pairs)  76.7 us
    unnamed x49, local copies, waits for them, and re-layouts  20.3 us
    ppermute x16, waiting for transfers between devices, from_behind(): return lax.ppermute(value, axis, pairs)  20.2 us
  transfers between devices with their start and end apart: 23, of which 10 were waited for; matrix products, arithmetic and copies ran while one was open for 4% of the time, Pallas kernels for 0%

commit v1 on v0

--- a/solution.py
+++ b/solution.py
@@ -226,7 +226,9 @@
     term_conv = jnp.einsum("shtk,shct->kc", patches, grad_pre, precision=HIGH)
     term_bias = jnp.sum(grad_pre, axis=(0, 1, 3))
     small = (term_conv, term_bias, jnp.stack(mix_terms), term_embed, term_gain)
-    flat_small = lax.psum(jnp.concatenate([t.reshape(-1) for t in small]), ("sims", "sites"))
+    flat_small = lax.psum(
+        lax.psum(jnp.concatenate([t.reshape(-1) for t in small]), "sims"), "sites"
+    )
     pieces = []
     lower = 0
     for t in small:

time: 870 us -> 634 us (0.73)
  waiting for transfers between devices: 684 us -> 439 us
    psum x1 -> x0, waiting for transfers between devices: 267 us -> none  [per_device(): lax.psum(jnp.concatenate([t.reshape(-1) for t in small]), ('sims', 'sites'))]
    unnamed x5 -> x4, waiting for transfers between devices: 386 us -> 418 us
    unnamed x49 -> x51, local copies, waits for them, and re-layouts: 20.3 us -> 19.2 us
  transfers between devices with their start and end apart: 23 -> 22, of which waited for: 10 -> 8; matrix products, arithmetic and copies ran while one was open for 4% -> 3% of each run, Pallas kernels for 0% -> 0%
where the time goes in v1:
time: 634 us; the launch traced here: 632 us
  waiting for transfers between devices  439 us (69%)
  starting transfers between devices  110 us (17%)
  local copies, waits for them, and re-layouts  35.8 us (6%)
  matrix products  21.3 us (3%)
  between operations  17.1 us (3%)
  other arithmetic  9.77 us (2%)
    unnamed x4, waiting for transfers between devices  418 us
    ppermute x16, starting transfers between devices, from_behind(): return lax.ppermute(value, axis, pairs)  83.2 us
    unnamed x51, local copies, waits for them, and re-layouts  19.2 us
    ppermute x2, starting transfers between devices, extended(): lax.ppermute(head, axis, [((i + 1) % count, i) for i in range(count)])  15.3 us
    ppermute x16, waiting for transfers between devices, from_behind(): return lax.ppermute(value, axis, pairs)  14.6 us
  transfers between devices with their start and end apart: 22, of which 8 were waited for; matrix products, arithmetic and copies ran while one was open for 3% of the time, Pallas kernels for 0%

profile of v1, /device:TPU:8, one launch (start us, length us, event | category | flops | bytes accessed | tf_op | source)
XLA Modules:
  0.0 632.4 jit_solution(18063071305196378591)
XLA Ops:
  9.1 4.5 fusion.16
  13.7 13.1 %collective-permute-start.1 = (f32[1,64,1]{2,1,0:T(8,128)S(1)}, f32[1,64,1]{2,1,0:T(8,128)S(1)}, u32[]{:S(2)}, u32[]{:S(2)}) collective-permute-start(f32[1,64,1]{2,1,0:T(8,128)S(1)} %get-tuple-element.35), channel_id=1, source_target_pairs={{1,0},{2,1},{3,2},{4,3},{5,4},{6,5},{7,6},{8,7},{9,8},{10,9},{11,1... | collective-permute-start | bytes 776 | tf_op jit(solution)/shard_map/ppermute | solution.py:22
  26.9 1.9 collective-permute-start
  30.9 6.0 collective-permute-done
  39.1 2.1 collective-permute-start.2
  41.7 4.6 collective-permute-start.3
  46.3 1.9 collective-permute-start.4
  48.3 7.8 %collective-permute-start.5 = (bf16[1,128,1025]{2,1,0:T(8,128)(2,1)}, bf16[1,128,1025]{2,1,0:T(8,128)(2,1)}, u32[]{:S(2)}, u32[]{:S(2)}) collective-permute-start(bf16[1,128,1025]{2,1,0:T(8,128)(2,1)} %get-tuple-element.32), channel_id=1, source_target_pairs={{0,2},{1,3},{2,4},{3,5},{4,6},{5,7},{6,8},{7,9},{8,10},{9,11},{10,... | collective-permute-start | bytes 787208 | tf_op jit(solution)/shard_map/ppermute | solution.py:32
  56.1 1.9 collective-permute-start.6
  58.4 6.0 collective-permute-start.7
  66.2 3.6 collective-permute-done.3
  69.7 4.6 collective-permute-start.8
  76.0 3.6 collective-permute-done.4
  79.7 16.0 %collective-permute-start.9 = (bf16[1,128,1025]{2,1,0:T(8,128)(2,1)}, bf16[1,128,1025]{2,1,0:T(8,128)(2,1)S(1)}, u32[]{:S(2)}, u32[]{:S(2)}) collective-permute-start(bf16[1,128,1025]{2,1,0:T(8,128)(2,1)} %get-tuple-element.32), channel_id=1, source_target_pairs={{0,4},{1,5},{2,6},{3,7},{4,8},{5,9},{6,10},{7,11},{8,12},{9,13},{1... | collective-permute-start | bytes 787208 | tf_op jit(solution)/shard_map/ppermute | solution.py:32
  103.3 2.8 fusion.114
  110.5 1.8 fusion.119
  117.7 6.1 collective-permute-start.10
  123.9 4.1 collective-permute-start.11
  128.0 4.2 collective-permute-start.12
  132.2 7.7 %collective-permute-start.13 = (bf16[1,128,16,64]{1,3,2,0:T(8,128)(2,1)S(1)}, bf16[1,128,16,64]{1,3,2,0:T(8,128)(2,1)S(1)}, u32[]{:S(2)}, u32[]{:S(2)}) collective-permute-start(bf16[1,128,16,64]{1,3,2,0:T(8,128)(2,1)S(1)} %pad_maximum_fusion.5), channel_id=1, source_target_pairs={{0,14},{1,15},{2,0},{3,1},{4,2},{5,3},{6,4},{7,5},{8,6},{9,7},{10,... | collective-permute-start | bytes 786440 | tf_op jit(solution)/shard_map/ppermute | solution.py:32
  140.0 2.1 collective-permute-start.14
  142.5 6.9 %collective-permute-start.15 = (bf16[1,128,16,64]{1,3,2,0:T(8,128)(2,1)S(1)}, bf16[1,128,16,64]{1,3,2,0:T(8,128)(2,1)S(1)}, u32[]{:S(2)}, u32[]{:S(2)}) collective-permute-start(bf16[1,128,16,64]{1,3,2,0:T(8,128)(2,1)S(1)} %pad_maximum_fusion.7), channel_id=1, source_target_pairs={{0,13},{1,14},{2,15},{3,0},{4,1},{5,2},{6,3},{7,4},{8,5},{9,6},{10... | collective-permute-start | bytes 786440 | tf_op jit(solution)/shard_map/ppermute | solution.py:32
  149.4 1.9 collective-permute-start.16
  151.4 5.1 collective-permute-start.17
  157.2 2.7 collective-permute-done.13
  160.0 4.5 collective-permute-done.14
  172.6 9.4 %collective-permute-start.19 = (bf16[1,64,1]{2,1,0:T(8,128)(2,1)}, bf16[1,64,1]{2,1,0:T(8,128)(2,1)S(1)}, u32[]{:S(2)}, u32[]{:S(2)}) collective-permute-start(bf16[1,64,1]{2,1,0:T(8,128)(2,1)} %get-tuple-element.37), channel_id=1, source_target_pairs={{0,1},{1,2},{2,3},{3,4},{4,5},{5,6},{6,7},{7,8},{8,9},{9,10},{10,1... | collective-permute-start | bytes 392 | tf_op jit(solution)/shard_map/ppermute | solution.py:20
  182.0 2.1 collective-permute-start.18
  185.8 3.1 copy.52
  190.4 2.4 fusion.30
  195.7 248.9 %all-reduce.7.cloned.1.call-done = (f32[1048576]{0:T(1024)}, f32[45888]{0:T(1024)}) async-done(((f32[1048576]{0:T(1024)}, f32[45888]{0:T(1024)}), (f32[1048576]{0:T(1024)}, f32[45888]{0:T(1024)})) %all-reduce.7.cloned.1.call-update) | async-done | bytes 4377872
  448.1 168.9 %all-reduce.9.cloned.1.call-done = (f32[32768]{0:T(1024)}, f32[45888]{0:T(1024)}) async-done(((f32[32768]{0:T(1024)}, f32[45888]{0:T(1024)}), (f32[32768]{0:T(1024)}, f32[45888]{0:T(1024)})) %all-reduce.9.cloned.1.call-update) | async-done | bytes 314640
  (161 shorter events, 52.6 us)
Async XLA Ops:
  7.2 30.0 %copy-start = (f32[64,512]{1,0:T(8,128)S(1)}, f32[64,512]{1,0:T(8,128)}, u32[]{:S(2)}) copy-start(f32[64,512]{1,0:T(8,128)} %param.17) | copy-start | bytes 393220
  7.2 437.4 %all-reduce.7.cloned.1.call-start = ((), (), s32[]{:S(2)}) async-start(), calls=%async_computation | async-start | bytes 8757248
  9.1 21.1 %copy-start.6 = (f32[3,64,64]{2,1,0:T(8,128)S(1)}, f32[3,64,64]{2,1,0:T(8,128)}, u32[]{:S(2)}) copy-start(f32[3,64,64]{2,1,0:T(8,128)} %param.16) | copy-start | bytes 147460
  9.1 21.3 %copy-start.17 = (bf16[1,128]{1,0:T(2,128)(2,1)S(1)}, bf16[1,128]{1,0:T(2,128)(2,1)}, u32[]{:S(2)}) copy-start(bf16[1,128]{1,0:T(2,128)(2,1)} %param.11) | copy-start | bytes 772
  9.1 28.6 %copy-start.14 = (f32[512]{0:T(512)S(1)}, f32[512]{0:T(512)}, u32[]{:S(2)}) copy-start(f32[512]{0:T(512)} %param.18) | copy-start | bytes 6148
  9.1 28.7 %copy-start.1 = (bf16[4,512,512]{2,1,0:T(8,128)(2,1)S(1)}, bf16[4,512,512]{2,1,0:T(8,128)(2,1)}, u32[]{:S(2)}) copy-start(bf16[4,512,512]{2,1,0:T(8,128)(2,1)} %param.19) | copy-start | bytes 6291460
  13.6 27.6 %copy-start.4 = (bf16[1,128,512]{2,1,0:T(8,128)(2,1)S(1)}, bf16[1,128,512]{2,1,0:T(8,128)(2,1)}, u32[]{:S(2)}) copy-start(bf16[1,128,512]{2,1,0:T(8,128)(2,1)} %param.13) | copy-start | bytes 393220
  13.7 16.8 %collective-permute-start.1 = (f32[1,64,1]{2,1,0:T(8,128)S(1)}, f32[1,64,1]{2,1,0:T(8,128)S(1)}, u32[]{:S(2)}, u32[]{:S(2)}) collective-permute-start(f32[1,64,1]{2,1,0:T(8,128)S(1)} %get-tuple-element.35), channel_id=1, source_target_pairs={{1,0},{2,1},{3,2},{4,3},{5,4},{6,5},{7,6},{8,7},{9,8},{10,9},{11,1... | collective-permute-start | bytes 776 | tf_op jit(solution)/shard_map/ppermute | solution.py:22
  26.9 10.0 %collective-permute-start = (f32[1,64,1]{2,1,0:T(8,128)S(1)}, f32[1,64,1]{2,1,0:T(8,128)S(1)}, u32[]{:S(2)}, u32[]{:S(2)}) collective-permute-start(f32[1,64,1]{2,1,0:T(8,128)S(1)} %get-tuple-element.34), channel_id=1, source_target_pairs={{0,1},{1,2},{2,3},{3,4},{4,5},{5,6},{6,7},{7,8},{8,9},{9,10},{10,1... | collective-permute-start | bytes 776 | tf_op jit(solution)/shard_map/ppermute | solution.py:20
  36.9 21.1 %copy-start.12 = (f32[1,64,1]{2,1,0:T(8,128)}, f32[1,64,1]{2,1,0:T(8,128)S(1)}, u32[]{:S(2)}) copy-start(f32[1,64,1]{2,1,0:T(8,128)S(1)} %collective-permute-done) | copy-start | bytes 772
  39.1 19.3 %collective-permute-start.2 = (bf16[1,128,1025]{2,1,0:T(8,128)(2,1)}, bf16[1,128,1025]{2,1,0:T(8,128)(2,1)}, u32[]{:S(2)}, u32[]{:S(2)}) collective-permute-start(bf16[1,128,1025]{2,1,0:T(8,128)(2,1)} %get-tuple-element.32), channel_id=1, source_target_pairs={{0,15},{1,0},{2,1},{3,2},{4,3},{5,4},{6,5},{7,6},{8,7},{9,8},{10,9... | collective-permute-start | bytes 787208 | tf_op jit(solution)/shard_map/ppermute | solution.py:32
  41.7 28.0 %collective-permute-start.3 = (bf16[1,128,1025]{2,1,0:T(8,128)(2,1)}, bf16[1,128,1025]{2,1,0:T(8,128)(2,1)}, u32[]{:S(2)}, u32[]{:S(2)}) collective-permute-start(bf16[1,128,1025]{2,1,0:T(8,128)(2,1)} %get-tuple-element.32), channel_id=1, source_target_pairs={{0,1},{1,2},{2,3},{3,4},{4,5},{5,6},{6,7},{7,8},{8,9},{9,10},{10,1... | collective-permute-start | bytes 787208 | tf_op jit(solution)/shard_map/ppermute | solution.py:32
  46.3 33.3 %collective-permute-start.4 = (bf16[1,128,1025]{2,1,0:T(8,128)(2,1)}, bf16[1,128,1025]{2,1,0:T(8,128)(2,1)}, u32[]{:S(2)}, u32[]{:S(2)}) collective-permute-start(bf16[1,128,1025]{2,1,0:T(8,128)(2,1)} %get-tuple-element.32), channel_id=1, source_target_pairs={{0,14},{1,15},{2,0},{3,1},{4,2},{5,3},{6,4},{7,5},{8,6},{9,7},{10,... | collective-permute-start | bytes 787208 | tf_op jit(solution)/shard_map/ppermute | solution.py:32
  48.3 49.2 %collective-permute-start.5 = (bf16[1,128,1025]{2,1,0:T(8,128)(2,1)}, bf16[1,128,1025]{2,1,0:T(8,128)(2,1)}, u32[]{:S(2)}, u32[]{:S(2)}) collective-permute-start(bf16[1,128,1025]{2,1,0:T(8,128)(2,1)} %get-tuple-element.32), channel_id=1, source_target_pairs={{0,2},{1,3},{2,4},{3,5},{4,6},{5,7},{6,8},{7,9},{8,10},{9,11},{10,... | collective-permute-start | bytes 787208 | tf_op jit(solution)/shard_map/ppermute | solution.py:32
  56.1 43.0 %collective-permute-start.6 = (bf16[1,128,1025]{2,1,0:T(8,128)(2,1)}, bf16[1,128,1025]{2,1,0:T(8,128)(2,1)}, u32[]{:S(2)}, u32[]{:S(2)}) collective-permute-start(bf16[1,128,1025]{2,1,0:T(8,128)(2,1)} %get-tuple-element.32), channel_id=1, source_target_pairs={{0,13},{1,14},{2,15},{3,0},{4,1},{5,2},{6,3},{7,4},{8,5},{9,6},{10... | collective-permute-start | bytes 787208 | tf_op jit(solution)/shard_map/ppermute | solution.py:32
  58.4 42.4 %collective-permute-start.7 = (bf16[1,128,1025]{2,1,0:T(8,128)(2,1)}, bf16[1,128,1025]{2,1,0:T(8,128)(2,1)S(1)}, u32[]{:S(2)}, u32[]{:S(2)}) collective-permute-start(bf16[1,128,1025]{2,1,0:T(8,128)(2,1)} %get-tuple-element.32), channel_id=1, source_target_pairs={{0,3},{1,4},{2,5},{3,6},{4,7},{5,8},{6,9},{7,10},{8,11},{9,12},{10... | collective-permute-start | bytes 787208 | tf_op jit(solution)/shard_map/ppermute | solution.py:32
  69.7 31.9 %collective-permute-start.8 = (bf16[1,128,1025]{2,1,0:T(8,128)(2,1)}, bf16[1,128,1025]{2,1,0:T(8,128)(2,1)S(1)}, u32[]{:S(2)}, u32[]{:S(2)}) collective-permute-start(bf16[1,128,1025]{2,1,0:T(8,128)(2,1)} %get-tuple-element.32), channel_id=1, source_target_pairs={{0,12},{1,13},{2,14},{3,15},{4,0},{5,1},{6,2},{7,3},{8,4},{9,5},{1... | collective-permute-start | bytes 787208 | tf_op jit(solution)/shard_map/ppermute | solution.py:32
  79.7 22.9 %collective-permute-start.9 = (bf16[1,128,1025]{2,1,0:T(8,128)(2,1)}, bf16[1,128,1025]{2,1,0:T(8,128)(2,1)S(1)}, u32[]{:S(2)}, u32[]{:S(2)}) collective-permute-start(bf16[1,128,1025]{2,1,0:T(8,128)(2,1)} %get-tuple-element.32), channel_id=1, source_target_pairs={{0,4},{1,5},{2,6},{3,7},{4,8},{5,9},{6,10},{7,11},{8,12},{9,13},{1... | collective-permute-start | bytes 787208 | tf_op jit(solution)/shard_map/ppermute | solution.py:32
  117.7 24.7 %collective-permute-start.10 = (bf16[1,128,16,64]{1,3,2,0:T(8,128)(2,1)S(1)}, bf16[1,128,16,64]{1,3,2,0:T(8,128)(2,1)S(1)}, u32[]{:S(2)}, u32[]{:S(2)}) collective-permute-start(bf16[1,128,16,64]{1,3,2,0:T(8,128)(2,1)S(1)} %pad_maximum_fusion.2), channel_id=1, source_target_pairs={{0,1},{1,2},{2,3},{3,4},{4,5},{5,6},{6,7},{7,8},{8,9},{9,10},{10,1... | collective-permute-start | bytes 786440 | tf_op jit(solution)/shard_map/ppermute | solution.py:32
  123.8 32.7 %copy-start.5 = (bf16[1,128,512]{2,1,0:T(8,128)(2,1)S(1)}, bf16[1,128,512]{2,1,0:T(8,128)(2,1)}, u32[]{:S(2)}) copy-start(bf16[1,128,512]{2,1,0:T(8,128)(2,1)} %param.13) | copy-start | bytes 393220
  123.9 25.6 %collective-permute-start.11 = (bf16[1,128,16,64]{1,3,2,0:T(8,128)(2,1)S(1)}, bf16[1,128,16,64]{1,3,2,0:T(8,128)(2,1)S(1)}, u32[]{:S(2)}, u32[]{:S(2)}) collective-permute-start(bf16[1,128,16,64]{1,3,2,0:T(8,128)(2,1)S(1)} %pad_maximum_fusion.3), channel_id=1, source_target_pairs={{0,15},{1,0},{2,1},{3,2},{4,3},{5,4},{6,5},{7,6},{8,7},{9,8},{10,9... | collective-permute-start | bytes 786440 | tf_op jit(solution)/shard_map/ppermute | solution.py:32
  128.0 23.3 %collective-permute-start.12 = (bf16[1,128,16,64]{1,3,2,0:T(8,128)(2,1)S(1)}, bf16[1,128,16,64]{1,3,2,0:T(8,128)(2,1)S(1)}, u32[]{:S(2)}, u32[]{:S(2)}) collective-permute-start(bf16[1,128,16,64]{1,3,2,0:T(8,128)(2,1)S(1)} %pad_maximum_fusion.4), channel_id=1, source_target_pairs={{0,2},{1,3},{2,4},{3,5},{4,6},{5,7},{6,8},{7,9},{8,10},{9,11},{10,... | collective-permute-start | bytes 786440 | tf_op jit(solution)/shard_map/ppermute | solution.py:32
  132.2 27.7 %collective-permute-start.13 = (bf16[1,128,16,64]{1,3,2,0:T(8,128)(2,1)S(1)}, bf16[1,128,16,64]{1,3,2,0:T(8,128)(2,1)S(1)}, u32[]{:S(2)}, u32[]{:S(2)}) collective-permute-start(bf16[1,128,16,64]{1,3,2,0:T(8,128)(2,1)S(1)} %pad_maximum_fusion.5), channel_id=1, source_target_pairs={{0,14},{1,15},{2,0},{3,1},{4,2},{5,3},{6,4},{7,5},{8,6},{9,7},{10,... | collective-permute-start | bytes 786440 | tf_op jit(solution)/shard_map/ppermute | solution.py:32
  139.9 16.9 %copy-start.2 = (bf16[4,512,512]{2,1,0:T(8,128)(2,1)S(1)}, bf16[4,512,512]{2,1,0:T(8,128)(2,1)}, u32[]{:S(2)}) copy-start(bf16[4,512,512]{2,1,0:T(8,128)(2,1)} %param.19) | copy-start | bytes 6291460
  140.0 24.5 %collective-permute-start.14 = (bf16[1,128,16,64]{1,3,2,0:T(8,128)(2,1)S(1)}, bf16[1,128,16,64]{1,3,2,0:T(8,128)(2,1)S(1)}, u32[]{:S(2)}, u32[]{:S(2)}) collective-permute-start(bf16[1,128,16,64]{1,3,2,0:T(8,128)(2,1)S(1)} %pad_maximum_fusion.6), channel_id=1, source_target_pairs={{0,3},{1,4},{2,5},{3,6},{4,7},{5,8},{6,9},{7,10},{8,11},{9,12},{10... | collective-permute-start | bytes 786440 | tf_op jit(solution)/shard_map/ppermute | solution.py:32
  142.5 22.1 %collective-permute-start.15 = (bf16[1,128,16,64]{1,3,2,0:T(8,128)(2,1)S(1)}, bf16[1,128,16,64]{1,3,2,0:T(8,128)(2,1)S(1)}, u32[]{:S(2)}, u32[]{:S(2)}) collective-permute-start(bf16[1,128,16,64]{1,3,2,0:T(8,128)(2,1)S(1)} %pad_maximum_fusion.7), channel_id=1, source_target_pairs={{0,13},{1,14},{2,15},{3,0},{4,1},{5,2},{6,3},{7,4},{8,5},{9,6},{10... | collective-permute-start | bytes 786440 | tf_op jit(solution)/shard_map/ppermute | solution.py:32
  149.4 15.2 %collective-permute-start.16 = (bf16[1,128,16,64]{1,3,2,0:T(8,128)(2,1)S(1)}, bf16[1,128,16,64]{1,3,2,0:T(8,128)(2,1)S(1)}, u32[]{:S(2)}, u32[]{:S(2)}) collective-permute-start(bf16[1,128,16,64]{1,3,2,0:T(8,128)(2,1)S(1)} %pad_maximum_fusion.8), channel_id=1, source_target_pairs={{0,4},{1,5},{2,6},{3,7},{4,8},{5,9},{6,10},{7,11},{8,12},{9,13},{1... | collective-permute-start | bytes 786440 | tf_op jit(solution)/shard_map/ppermute | solution.py:32
  151.4 13.3 %collective-permute-start.17 = (bf16[1,128,16,64]{1,3,2,0:T(8,128)(2,1)S(1)}, bf16[1,128,16,64]{1,3,2,0:T(8,128)(2,1)S(1)}, u32[]{:S(2)}, u32[]{:S(2)}) collective-permute-start(bf16[1,128,16,64]{1,3,2,0:T(8,128)(2,1)S(1)} %pad_maximum_fusion.9), channel_id=1, source_target_pairs={{0,12},{1,13},{2,14},{3,15},{4,0},{5,1},{6,2},{7,3},{8,4},{9,5},{1... | collective-permute-start | bytes 786440 | tf_op jit(solution)/shard_map/ppermute | solution.py:32
  166.5 4.9 copy-start.13
  172.6 16.3 %collective-permute-start.19 = (bf16[1,64,1]{2,1,0:T(8,128)(2,1)}, bf16[1,64,1]{2,1,0:T(8,128)(2,1)S(1)}, u32[]{:S(2)}, u32[]{:S(2)}) collective-permute-start(bf16[1,64,1]{2,1,0:T(8,128)(2,1)} %get-tuple-element.37), channel_id=1, source_target_pairs={{0,1},{1,2},{2,3},{3,4},{4,5},{5,6},{6,7},{7,8},{8,9},{9,10},{10,1... | collective-permute-start | bytes 392 | tf_op jit(solution)/shard_map/ppermute | solution.py:20
  182.0 7.2 %collective-permute-start.18 = (bf16[1,64,1]{2,1,0:T(8,128)(2,1)}, bf16[1,64,1]{2,1,0:T(8,128)(2,1)S(1)}, u32[]{:S(2)}, u32[]{:S(2)}) collective-permute-start(bf16[1,64,1]{2,1,0:T(8,128)(2,1)} %get-tuple-element.36), channel_id=1, source_target_pairs={{1,0},{2,1},{3,2},{4,3},{5,4},{6,5},{7,6},{8,7},{9,8},{10,9},{11,1... | collective-permute-start | bytes 392 | tf_op jit(solution)/shard_map/ppermute | solution.py:22
  193.7 423.3 %all-reduce.9.cloned.1.call-start = ((), (), s32[]{:S(2)}) async-start(), calls=%async_computation.1 | async-start | bytes 630784
  (9 other events, 21.6 us)
Sparse Core Ops, SparseCore 0:
  193.8 250.7 all-reduce.6
  448.4 168.5 all-reduce.8
